TPU v7x, 512 devices: a whole 4x4x16 slice. The times are simulated.
512 devices in a mesh: tiles: 128 (over y, z, core), samp: 4 (over x).
Axes of the slice: x: 4, y: 4, z: 16, core: 2. Of those that a mesh axis runs over, the one named last changes fastest.
Arguments:
- samples: bfloat16 [256, 131072], P('samp', 'tiles'), may hold values from -6 to 6
- omega: float32 [1280, 512, 512], P('tiles', 'samp'), may hold values from -1 to 2, as said below
- coords: int32 [1280, 2], P('tiles'), may hold values from 0 to 255, as said below
Outputs:
- updated: float32 [1280, 512, 512], P('tiles', 'samp')
Inputs may be any that keep to these rules, and one draw needn't show every extreme that they name: `coords`: tile k lies with index k // 10 of tiles. Write d for that index, and blocks d * 2 to (d + 1) * 2 - 1 as its own blocks; indices of devices wrap around. The first 2 tiles of d are the diagonal tiles (I, I) of its own blocks in order. Each other tile of d is (I, J) with I an own block and J a block of d + 1, or I a block of d - 1 and J a block of d + 1, or I < J both own blocks. No unordered pair of blocks appears twice in the whole list. `omega`: tiles with I == J are symmetric with diagonal entries from 0.5 to 2.
All inputs are finite; a program needn't handle non-finite values.
Results may differ from a plain program's by a relative error of at most 0.0023.
Values may be sent and summed in bfloat16 or wider, within the bound.
No kernel may reach another device: no remote copies, remote signals or barrier semaphores. Data moves between devices by JAX's collectives and lax.ppermute only.
A program may use at most 64 MiB of HBM per device.

v0:
```python
import jax
import jax.numpy as jnp
from jax import lax
from jax.sharding import PartitionSpec as P

BLK_DEV = 2
ITERS = 2
step_size = 0.25
penalty = 0.2


def with_halo(shard, sides, width):
    for axis, dim in sides:
        size, length = (lax.axis_size(axis), shard.shape[dim])
        up = [(i, (i + 1) % size) for i in range(size)]
        down = [(j, i) for i, j in up]
        last = lax.slice_in_dim(shard, length - width, length, axis=dim)
        leading = lax.slice_in_dim(shard, 0, width, axis=dim)
        before = lax.ppermute(last, axis, up)
        after = lax.ppermute(leading, axis, down)
        shard = jnp.concatenate([before, shard, after], axis=dim)
    return shard


def columns(matrix, start, count):
    return lax.dynamic_slice_in_dim(matrix, start, count, 1)


def add_columns(totals, block, start):
    current = lax.dynamic_slice_in_dim(totals, start, block.shape[1], 1)
    return lax.dynamic_update_slice_in_dim(totals, current + block, start, 1)


def shards(samples, omega, coords):
    quarter = lax.axis_index("samp")
    tile_rows = omega.shape[1]
    width = omega.shape[2]
    own_width = samples.shape[1]
    blocks_all = BLK_DEV * lax.axis_size("tiles")
    first_block = (lax.axis_index("tiles") - 1) * BLK_DEV
    local = (coords - first_block + blocks_all) % blocks_all
    off_diagonal = (coords[:, 0] != coords[:, 1]).astype(jnp.float32)
    offset = quarter * tile_rows
    full_rows = lax.all_gather(samples, "samp", axis=0, tiled=True)
    sample_win = with_halo(full_rows, (("tiles", 1),), own_width)
    count = sample_win.shape[0]
    row_ids = offset + lax.broadcasted_iota(jnp.int32, (tile_rows, width), 0)
    col_ids = lax.broadcasted_iota(jnp.int32, (tile_rows, width), 1)
    diagonal_cells = row_ids == col_ids
    contract_cols = (((1,), (1,)), ((), ()))
    contract_rows = (((0,), (0,)), ((), ()))
    for iteration in range(ITERS):
        omega_low = omega.astype(jnp.bfloat16)
        totals = jnp.zeros((count, 3 * own_width), jnp.float32)
        for tile_slot in range(omega.shape[0]):
            row_start = local[tile_slot, 0] * width
            col_start = local[tile_slot, 1] * width
            rows_low = omega_low[tile_slot]
            row_part = columns(sample_win, row_start + offset, tile_rows)
            col_block = columns(sample_win, col_start, width)
            to_col = jnp.dot(row_part, rows_low, preferred_element_type=jnp.float32)
            to_row = lax.dot_general(
                col_block, rows_low, contract_cols, preferred_element_type=jnp.float32
            )
            totals = add_columns(totals, to_col, col_start)
            totals = add_columns(totals, to_row * off_diagonal[tile_slot], row_start + offset)
        returned = with_halo(totals, (("tiles", 1),), own_width)
        partial_value = (
            totals[:, own_width : 2 * own_width]
            + returned[:, :own_width]
            + returned[:, 4 * own_width :]
        )
        summed = lax.psum(partial_value, "samp")
        product_own = summed.astype(jnp.bfloat16)
        product_win = with_halo(product_own, (("tiles", 1),), own_width)
        new_tiles = []
        for tile_slot in range(omega.shape[0]):
            row_start = local[tile_slot, 0] * width
            col_start = local[tile_slot, 1] * width
            product_rows = columns(product_win, row_start + offset, tile_rows)
            sample_rows = columns(sample_win, row_start + offset, tile_rows)
            sample_cols = columns(sample_win, col_start, width)
            product_cols = columns(product_win, col_start, width)
            first = lax.dot_general(
                product_rows, sample_cols, contract_rows, preferred_element_type=jnp.float32
            )
            second = lax.dot_general(
                sample_rows, product_cols, contract_rows, preferred_element_type=jnp.float32
            )
            grad = (first + second) / (2.0 * count)
            value = omega[tile_slot] - step_size * grad
            shrunk = jnp.sign(value) * jnp.maximum(jnp.abs(value) - step_size * penalty, 0.0)
            positive = 0.5 * (value + jnp.sqrt(value * value + 4.0 * step_size))
            same_block = coords[tile_slot, 0] == coords[tile_slot, 1]
            new_tiles.append(jnp.where(diagonal_cells & same_block, positive, shrunk))
        omega = jnp.stack(new_tiles)
    return omega


def solution(mesh):
    in_specs = (P("samp", "tiles"), P("tiles", "samp", None), P("tiles", None))
    out_specs = P("tiles", "samp", None)
    return jax.shard_map(shards, mesh=mesh, in_specs=in_specs, out_specs=out_specs, check_vma=False)
```

profile of v0, /device:TPU:4, one launch (start us, length us, event | category | flops | bytes accessed | tf_op | source)
XLA Modules:
  0.0 228.5 jit_solution(8097895202772696019)
XLA Ops:
  0.0 16.8 %all_gather.3 = bf16[256,1024]{1,0:T(8,128)(2,1)S(1)} all-gather(bf16[64,1024]{1,0:T(8,128)(2,1)} %param.3), channel_id=1, replica_groups=mesh['tiles'=128,'samp'=4] {'samp'}, dimensions={0}, use_global_device_ids=true | all-gather | bytes 655360 | tf_op jit(solution)/shard_map/all_gather | solution.py:44
  16.8 1.9 collective-permute-start
  18.7 7.0 %collective-permute-start.1 = (bf16[256,1024]{1,0:T(8,128)(2,1)S(1)}, bf16[256,1024]{1,0:T(8,128)(2,1)}, u32[]{:S(2)}, u32[]{:S(2)}) collective-permute-start(bf16[256,1024]{1,0:T(8,128)(2,1)S(1)} %all_gather.3), channel_id=1, source_target_pairs={{4,0},{8,4},{12,8},{16,12},{20,16},{24,20},{28,24},{32,28},{36,32}... | collective-permute-start | bytes 1572872 | tf_op jit(solution)/shard_map/ppermute | solution.py:20
  25.7 0.7 and_select_fusion
  26.4 0.6 slice.169
  26.9 0.7 fusion.374
  40.3 1.9 convert_element_type.14
  42.4 0.7 fusion.375
  43.1 1.1 constant_dynamic-update-slice_fusion.2
  44.2 1.1 constant_dynamic-update-slice_fusion
  45.9 0.9 add_dynamic-update-slice_fusion.19
  47.0 0.8 fusion.59
  48.0 0.8 add_dynamic-update-slice_fusion.18
  49.1 0.9 add_dynamic-update-slice_fusion.17
  50.2 0.8 add_dynamic-update-slice_fusion.16
  51.2 0.9 add_dynamic-update-slice_fusion.15
  52.4 0.9 add_dynamic-update-slice_fusion.14
  53.4 0.8 add_dynamic-update-slice_fusion.13
  54.5 0.8 add_dynamic-update-slice_fusion.12
  55.5 0.9 add_dynamic-update-slice_fusion.11
  56.7 1.9 collective-permute-start.2
  58.6 7.0 %collective-permute-start.3 = (f32[256,1024]{1,0:T(8,128)S(1)}, f32[256,1024]{1,0:T(8,128)S(1)}, u32[]{:S(2)}, u32[]{:S(2)}) collective-permute-start(f32[256,1024]{1,0:T(8,128)S(1)} %get-tuple-element.8), channel_id=1, source_target_pairs={{4,0},{8,4},{12,8},{16,12},{20,16},{24,20},{28,24},{32,28},{36,32}... | collective-permute-start | bytes 3145736 | tf_op jit(solution)/shard_map/ppermute | solution.py:20
  65.6 10.5 %collective-permute-done.2 = f32[256,1024]{1,0:T(8,128)S(1)} collective-permute-done((f32[256,1024]{1,0:T(8,128)S(1)}, f32[256,1024]{1,0:T(8,128)S(1)}, u32[]{:S(2)}, u32[]{:S(2)}) %collective-permute-start.2) | collective-permute-done | bytes 1048608 | tf_op jit(solution)/shard_map/ppermute | solution.py:19
  76.1 1.8 collective-permute-done.3
  78.2 28.7 %all-reduce.2 = bf16[256,1024]{1,0:T(8,128)(2,1)S(1)} all-reduce(f32[256,1024]{1,0:T(8,128)S(1)} %fusion.61), channel_id=1, replica_groups=mesh['tiles'=128,'samp'=4] {'samp'}, use_global_device_ids=true, to_apply=%region_0.1 | all-reduce | flops 262144 | bytes 1572864 | tf_op jit(solution)/shard_map/psum | solution.py:73
  106.9 1.9 collective-permute-start.4
  108.8 7.1 %collective-permute-start.5 = (bf16[256,1024]{1,0:T(8,128)(2,1)S(1)}, bf16[256,1024]{1,0:T(8,128)(2,1)S(1)}, u32[]{:S(2)}, u32[]{:S(2)}) collective-permute-start(bf16[256,1024]{1,0:T(8,128)(2,1)S(1)} %all-reduce.2), channel_id=1, source_target_pairs={{4,0},{8,4},{12,8},{16,12},{20,16},{24,20},{28,24},{32,28},{36,32}... | collective-permute-start | bytes 1572872 | tf_op jit(solution)/shard_map/ppermute | solution.py:20
  116.0 0.6 slice.416
  116.6 0.7 fusion.373
  132.2 0.6 copy-done
  133.9 0.9 add_dynamic-update-slice_fusion.10
  135.5 0.8 fusion.57
  136.3 0.5 multiply_select_fusion.7
  137.1 0.8 add_dynamic-update-slice_fusion.9
  138.7 0.9 add_dynamic-update-slice_fusion.8
  139.6 0.5 multiply_select_fusion.5
  140.3 0.8 add_dynamic-update-slice_fusion.7
  141.1 0.5 multiply_select_fusion.4
  141.9 0.9 add_dynamic-update-slice_fusion.6
  143.5 0.8 add_dynamic-update-slice_fusion.5
  144.4 0.5 multiply_select_fusion.2
  145.2 0.8 add_dynamic-update-slice_fusion.4
  145.9 0.5 multiply_select_fusion.1
  146.7 0.8 add_dynamic-update-slice_fusion.3
  148.8 0.9 add_dynamic-update-slice_fusion.2
  149.9 1.9 collective-permute-start.6
  151.9 7.0 %collective-permute-start.7 = (f32[256,1024]{1,0:T(8,128)S(1)}, f32[256,1024]{1,0:T(8,128)S(1)}, u32[]{:S(2)}, u32[]{:S(2)}) collective-permute-start(f32[256,1024]{1,0:T(8,128)S(1)} %get-tuple-element.6), channel_id=1, source_target_pairs={{4,0},{8,4},{12,8},{16,12},{20,16},{24,20},{28,24},{32,28},{36,32}... | collective-permute-start | bytes 3145736 | tf_op jit(solution)/shard_map/ppermute | solution.py:20
  158.8 10.5 %collective-permute-done.6 = f32[256,1024]{1,0:T(8,128)S(1)} collective-permute-done((f32[256,1024]{1,0:T(8,128)S(1)}, f32[256,1024]{1,0:T(8,128)S(1)}, u32[]{:S(2)}, u32[]{:S(2)}) %collective-permute-start.6) | collective-permute-done | bytes 1048608 | tf_op jit(solution)/shard_map/ppermute | solution.py:19
  169.4 1.8 collective-permute-done.7
  171.4 31.7 %all-reduce.3 = bf16[256,1024]{1,0:T(8,128)(2,1)S(1)} all-reduce(f32[256,1024]{1,0:T(8,128)S(1)} %fusion.60), channel_id=1, replica_groups=mesh['tiles'=128,'samp'=4] {'samp'}, use_global_device_ids=true, to_apply=%region_1.2 | all-reduce | flops 262144 | bytes 1572864 | tf_op jit(solution)/shard_map/psum | solution.py:73
  203.1 1.9 collective-permute-start.8
  205.1 7.2 %collective-permute-start.9 = (bf16[256,1024]{1,0:T(8,128)(2,1)S(1)}, bf16[256,1024]{1,0:T(8,128)(2,1)S(1)}, u32[]{:S(2)}, u32[]{:S(2)}) collective-permute-start(bf16[256,1024]{1,0:T(8,128)(2,1)S(1)} %all-reduce.3), channel_id=1, source_target_pairs={{4,0},{8,4},{12,8},{16,12},{20,16},{24,20},{28,24},{32,28},{36,32}... | collective-permute-start | bytes 1572872 | tf_op jit(solution)/shard_map/ppermute | solution.py:20
  212.2 4.7 %collective-permute-done.8 = bf16[256,1024]{1,0:T(8,128)(2,1)S(1)} collective-permute-done((bf16[256,1024]{1,0:T(8,128)(2,1)S(1)}, bf16[256,1024]{1,0:T(8,128)(2,1)S(1)}, u32[]{:S(2)}, u32[]{:S(2)}) %collective-permute-start.8) | collective-permute-done | bytes 524320 | tf_op jit(solution)/shard_map/ppermute | solution.py:19
  216.9 1.8 collective-permute-done.9
  221.1 0.5 bitcast_dynamic-update-slice_fusion.9
  221.6 0.5 bitcast_dynamic-update-slice_fusion.8
  222.2 0.5 bitcast_dynamic-update-slice_fusion.7
  222.7 0.5 bitcast_dynamic-update-slice_fusion.6
  223.2 0.5 bitcast_dynamic-update-slice_fusion.5
  223.7 0.5 bitcast_dynamic-update-slice_fusion.4
  224.8 0.5 bitcast_dynamic-update-slice_fusion.2
  225.3 0.5 bitcast_dynamic-update-slice_fusion.1
  225.8 1.5 copy-done.20
  227.3 1.2 bitcast_dynamic-update-slice_fusion
  (101 shorter events, 14.4 us)
Async XLA Ops:
  16.8 26.3 %collective-permute-start = (bf16[256,1024]{1,0:T(8,128)(2,1)S(1)}, bf16[256,1024]{1,0:T(8,128)(2,1)}, u32[]{:S(2)}, u32[]{:S(2)}) collective-permute-start(bf16[256,1024]{1,0:T(8,128)(2,1)S(1)} %all_gather.3), channel_id=1, source_target_pairs={{0,4},{4,8},{8,12},{12,16},{16,20},{20,24},{24,28},{28,32},{32,36}... | collective-permute-start | bytes 1572872 | tf_op jit(solution)/shard_map/ppermute | solution.py:19
  18.7 25.5 %collective-permute-start.1 = (bf16[256,1024]{1,0:T(8,128)(2,1)S(1)}, bf16[256,1024]{1,0:T(8,128)(2,1)}, u32[]{:S(2)}, u32[]{:S(2)}) collective-permute-start(bf16[256,1024]{1,0:T(8,128)(2,1)S(1)} %all_gather.3), channel_id=1, source_target_pairs={{4,0},{8,4},{12,8},{16,12},{20,16},{24,20},{28,24},{32,28},{36,32}... | collective-permute-start | bytes 1572872 | tf_op jit(solution)/shard_map/ppermute | solution.py:20
  40.3 2.1 copy-start.19
  56.7 19.4 %collective-permute-start.2 = (f32[256,1024]{1,0:T(8,128)S(1)}, f32[256,1024]{1,0:T(8,128)S(1)}, u32[]{:S(2)}, u32[]{:S(2)}) collective-permute-start(f32[256,1024]{1,0:T(8,128)S(1)} %get-tuple-element.7), channel_id=1, source_target_pairs={{0,4},{4,8},{8,12},{12,16},{16,20},{20,24},{24,28},{28,32},{32,36}... | collective-permute-start | bytes 3145736 | tf_op jit(solution)/shard_map/ppermute | solution.py:19
  58.6 19.3 %collective-permute-start.3 = (f32[256,1024]{1,0:T(8,128)S(1)}, f32[256,1024]{1,0:T(8,128)S(1)}, u32[]{:S(2)}, u32[]{:S(2)}) collective-permute-start(f32[256,1024]{1,0:T(8,128)S(1)} %get-tuple-element.8), channel_id=1, source_target_pairs={{4,0},{8,4},{12,8},{16,12},{20,16},{24,20},{28,24},{32,28},{36,32}... | collective-permute-start | bytes 3145736 | tf_op jit(solution)/shard_map/ppermute | solution.py:20
  106.9 22.9 %collective-permute-start.4 = (bf16[256,1024]{1,0:T(8,128)(2,1)S(1)}, bf16[256,1024]{1,0:T(8,128)(2,1)S(1)}, u32[]{:S(2)}, u32[]{:S(2)}) collective-permute-start(bf16[256,1024]{1,0:T(8,128)(2,1)S(1)} %all-reduce.2), channel_id=1, source_target_pairs={{0,4},{4,8},{8,12},{12,16},{16,20},{20,24},{24,28},{28,32},{32,36}... | collective-permute-start | bytes 1572872 | tf_op jit(solution)/shard_map/ppermute | solution.py:19
  108.8 21.0 %collective-permute-start.5 = (bf16[256,1024]{1,0:T(8,128)(2,1)S(1)}, bf16[256,1024]{1,0:T(8,128)(2,1)S(1)}, u32[]{:S(2)}, u32[]{:S(2)}) collective-permute-start(bf16[256,1024]{1,0:T(8,128)(2,1)S(1)} %all-reduce.2), channel_id=1, source_target_pairs={{4,0},{8,4},{12,8},{16,12},{20,16},{24,20},{28,24},{32,28},{36,32}... | collective-permute-start | bytes 1572872 | tf_op jit(solution)/shard_map/ppermute | solution.py:20
  131.1 1.7 copy-start
  135.2 1.6 copy-start.3
  136.9 1.5 copy-start.5
  138.4 1.7 copy-start.7
  140.1 1.5 copy-start.9
  141.6 1.7 copy-start.11
  143.3 1.6 copy-start.13
  144.9 1.5 copy-start.15
  146.5 1.6 copy-start.17
  148.1 0.7 copy-start.1
  149.9 19.4 %collective-permute-start.6 = (f32[256,1024]{1,0:T(8,128)S(1)}, f32[256,1024]{1,0:T(8,128)S(1)}, u32[]{:S(2)}, u32[]{:S(2)}) collective-permute-start(f32[256,1024]{1,0:T(8,128)S(1)} %get-tuple-element.5), channel_id=1, source_target_pairs={{0,4},{4,8},{8,12},{12,16},{16,20},{20,24},{24,28},{28,32},{32,36}... | collective-permute-start | bytes 3145736 | tf_op jit(solution)/shard_map/ppermute | solution.py:19
  151.9 19.3 %collective-permute-start.7 = (f32[256,1024]{1,0:T(8,128)S(1)}, f32[256,1024]{1,0:T(8,128)S(1)}, u32[]{:S(2)}, u32[]{:S(2)}) collective-permute-start(f32[256,1024]{1,0:T(8,128)S(1)} %get-tuple-element.6), channel_id=1, source_target_pairs={{4,0},{8,4},{12,8},{16,12},{20,16},{24,20},{28,24},{32,28},{36,32}... | collective-permute-start | bytes 3145736 | tf_op jit(solution)/shard_map/ppermute | solution.py:20
  203.1 13.8 %collective-permute-start.8 = (bf16[256,1024]{1,0:T(8,128)(2,1)S(1)}, bf16[256,1024]{1,0:T(8,128)(2,1)S(1)}, u32[]{:S(2)}, u32[]{:S(2)}) collective-permute-start(bf16[256,1024]{1,0:T(8,128)(2,1)S(1)} %all-reduce.3), channel_id=1, source_target_pairs={{0,4},{4,8},{8,12},{12,16},{16,20},{20,24},{24,28},{28,32},{32,36}... | collective-permute-start | bytes 1572872 | tf_op jit(solution)/shard_map/ppermute | solution.py:19
  205.1 13.6 %collective-permute-start.9 = (bf16[256,1024]{1,0:T(8,128)(2,1)S(1)}, bf16[256,1024]{1,0:T(8,128)(2,1)S(1)}, u32[]{:S(2)}, u32[]{:S(2)}) collective-permute-start(bf16[256,1024]{1,0:T(8,128)(2,1)S(1)} %all-reduce.3), channel_id=1, source_target_pairs={{4,0},{8,4},{12,8},{16,12},{20,16},{24,20},{28,24},{32,28},{36,32}... | collective-permute-start | bytes 1572872 | tf_op jit(solution)/shard_map/ppermute | solution.py:20
  220.4 1.2 copy-start.4
  220.9 1.3 copy-start.6
  221.6 1.0 copy-start.8
  222.1 1.0 copy-start.10
  222.7 1.0 copy-start.12
  223.2 1.0 copy-start.14
  223.7 1.0 copy-start.16
  224.2 1.0 copy-start.18
  224.8 2.5 %copy-start.2 = (f32[128,512]{1,0:T(8,128)S(1)}, f32[128,512]{1,0:T(8,128)}, u32[]{:S(2)}) copy-start(f32[128,512]{1,0:T(8,128)} %copy-done.1) | copy-start | bytes 786436
  225.8 1.5 copy-start.20
where the time goes:
time: 230 us; the launch traced here: 228 us
  blocking collectives  77.2 us (34%)
  starting transfers between devices  44.8 us (19%)
  matrix products  36.4 us (16%)
  waiting for transfers between devices  31.1 us (14%)
  between operations  26.3 us (11%)
  local copies, waits for them, and re-layouts  9.34 us (4%)
  other arithmetic  3.42 us (1%)
    psum x2, blocking collectives, shards(): summed = lax.psum(partial_value, 'samp')  60.4 us
    ppermute x5, starting transfers between devices, with_halo(): after = lax.ppermute(leading, axis, down)  35.2 us
    ppermute x5, waiting for transfers between devices, with_halo(): before = lax.ppermute(last, axis, up)  25.8 us
    dot_general x20, matrix products, shards(): lax.dot_general(col_block, rows_low, contract_cols, preferred_element_typ...  17 us
    all_gather x1, blocking collectives, shards(): full_rows = lax.all_gather(samples, 'samp', axis=0, tiled=True)  16.8 us
    dot_general x20, matrix products, shards(): lax.dot_general(product_rows, sample_cols, contract_rows, preferred_eleme...  10.6 us
    ppermute x5, starting transfers between devices, with_halo(): before = lax.ppermute(last, axis, up)  9.59 us
    ppermute x5, waiting for transfers between devices, with_halo(): after = lax.ppermute(leading, axis, down)  5.27 us
  transfers between devices with their start and end apart: 10, of which 6 were waited for; matrix products, arithmetic and copies ran while one was open for 3% of the time, Pallas kernels for 0%

commit v1 on v0

--- a/solution.py
+++ b/solution.py
@@ -41,7 +41,9 @@
     local = (coords - first_block + blocks_all) % blocks_all
     off_diagonal = (coords[:, 0] != coords[:, 1]).astype(jnp.float32)
     offset = quarter * tile_rows
-    full_rows = lax.all_gather(samples, "samp", axis=0, tiled=True)
+    full_rows = jnp.concatenate(
+        lax.all_to_all(jnp.stack([samples] * lax.axis_size("samp")), "samp", 0, 0), axis=0
+    )
     sample_win = with_halo(full_rows, (("tiles", 1),), own_width)
     count = sample_win.shape[0]
     row_ids = offset + lax.broadcasted_iota(jnp.int32, (tile_rows, width), 0)

time: 230 us -> 231 us (level)
  blocking collectives: 77.2 us -> 60.8 us
  starting transfers between devices: 44.8 us -> 56.2 us
  waiting for transfers between devices: 31.1 us -> 36.2 us
    all_gather x1 -> x0, blocking collectives: 16.8 us -> none  [shards(): full_rows = lax.all_gather(samples, 'samp', axis=0, tiled=True)]
    all_to_all x0 -> x1, starting transfers between devices: none -> 9.29 us  [shards(): lax.all_to_all(jnp.stack([samples] * lax.axis_size('samp')), 'samp', 0, 0)]
    all_to_all x0 -> x1, waiting for transfers between devices: none -> 5.12 us  [shards(): lax.all_to_all(jnp.stack([samples] * lax.axis_size('samp')), 'samp', 0, 0)]
  transfers between devices with their start and end apart: 10 -> 11, of which waited for: 6 -> 7; matrix products, arithmetic and copies ran while one was open for 3% -> 2% of each run, Pallas kernels for 0% -> 0%
where the time goes in v1:
time: 231 us; the launch traced here: 230 us
  blocking collectives  60.8 us (26%)
  starting transfers between devices  56.2 us (24%)
  matrix products  36.4 us (16%)
  waiting for transfers between devices  36.2 us (16%)
  between operations  26.3 us (11%)
  local copies, waits for them, and re-layouts  9.64 us (4%)
  other arithmetic  4.04 us (2%)
    psum x2, blocking collectives, shards(): summed = lax.psum(partial_value, 'samp')  60.8 us
    ppermute x5, starting transfers between devices, with_halo(): after = lax.ppermute(leading, axis, down)  37.3 us
    ppermute x5, waiting for transfers between devices, with_halo(): before = lax.ppermute(last, axis, up)  25.8 us
    dot_general x20, matrix products, shards(): lax.dot_general(col_block, rows_low, contract_cols, preferred_element_typ...  17 us
    dot_general x20, matrix products, shards(): lax.dot_general(product_rows, sample_cols, contract_rows, preferred_eleme...  10.6 us
    ppermute x5, starting transfers between devices, with_halo(): before = lax.ppermute(last, axis, up)  9.59 us
    all_to_all x1, starting transfers between devices, shards(): lax.all_to_all(jnp.stack([samples] * lax.axis_size('samp')), 'samp', 0, 0)  9.29 us
    ppermute x5, waiting for transfers between devices, with_halo(): after = lax.ppermute(leading, axis, down)  5.27 us
  transfers between devices with their start and end apart: 11, of which 7 were waited for; matrix products, arithmetic and copies ran while one was open for 2% of the time, Pallas kernels for 0%

profile of v1, /device:TPU:4, one launch (start us, length us, event | category | flops | bytes accessed | tf_op | source)
XLA Modules:
  0.0 229.6 jit_solution(14488314306919562)
XLA Ops:
  0.0 1.8 stack.62
  1.8 9.3 %all-to-all-start = ((bf16[4,64,1024]{2,1,0:T(8,128)(2,1)}), bf16[4,64,1024]{2,1,0:T(8,128)(2,1)S(1)}, u32[]{:S(2)}, u32[]{:S(2)}) async-start(bf16[4,64,1024]{2,1,0:T(8,128)(2,1)} %stack.62), calls=%async_computation | async-start | bytes 1048576 | tf_op jit(solution)/shard_map/all_to_all | solution.py:45
  11.1 5.1 %all-to-all-done = bf16[4,64,1024]{2,1,0:T(8,128)(2,1)S(1)} async-done(((bf16[4,64,1024]{2,1,0:T(8,128)(2,1)}), bf16[4,64,1024]{2,1,0:T(8,128)(2,1)S(1)}, u32[]{:S(2)}, u32[]{:S(2)}) %all-to-all-start) | async-done | bytes 524320 | tf_op jit(solution)/shard_map/all_to_all | solution.py:45
  16.2 1.9 collective-permute-start
  18.1 9.1 %collective-permute-start.1 = (bf16[256,1024]{1,0:T(8,128)(2,1)S(1)}, bf16[256,1024]{1,0:T(8,128)(2,1)}, u32[]{:S(2)}, u32[]{:S(2)}) collective-permute-start(bf16[256,1024]{1,0:T(8,128)(2,1)S(1)} %bitcast.162), channel_id=1, source_target_pairs={{4,0},{8,4},{12,8},{16,12},{20,16},{24,20},{28,24},{32,28},{36,32}... | collective-permute-start | bytes 1572872 | tf_op jit(solution)/shard_map/ppermute | solution.py:20
  27.2 0.5 slice.169
  27.7 0.7 fusion.374
  41.1 1.9 convert_element_type.14
  43.2 0.7 fusion.375
  43.9 0.8 copy-done.19
  44.7 1.3 pad_maximum_fusion
  46.6 0.9 add_dynamic-update-slice_fusion.19
  47.7 0.9 fusion.59
  48.8 0.8 add_dynamic-update-slice_fusion.18
  49.9 0.9 add_dynamic-update-slice_fusion.17
  51.0 0.8 add_dynamic-update-slice_fusion.16
  52.0 0.8 add_dynamic-update-slice_fusion.15
  53.1 0.9 add_dynamic-update-slice_fusion.14
  54.2 0.8 add_dynamic-update-slice_fusion.13
  55.2 0.9 add_dynamic-update-slice_fusion.12
  56.4 0.8 add_dynamic-update-slice_fusion.11
  57.4 1.9 collective-permute-start.2
  59.3 7.0 %collective-permute-start.3 = (f32[256,1024]{1,0:T(8,128)S(1)}, f32[256,1024]{1,0:T(8,128)S(1)}, u32[]{:S(2)}, u32[]{:S(2)}) collective-permute-start(f32[256,1024]{1,0:T(8,128)S(1)} %get-tuple-element.8), channel_id=1, source_target_pairs={{4,0},{8,4},{12,8},{16,12},{20,16},{24,20},{28,24},{32,28},{36,32}... | collective-permute-start | bytes 3145736 | tf_op jit(solution)/shard_map/ppermute | solution.py:20
  66.3 10.5 %collective-permute-done.2 = f32[256,1024]{1,0:T(8,128)S(1)} collective-permute-done((f32[256,1024]{1,0:T(8,128)S(1)}, f32[256,1024]{1,0:T(8,128)S(1)}, u32[]{:S(2)}, u32[]{:S(2)}) %collective-permute-start.2) | collective-permute-done | bytes 1048608 | tf_op jit(solution)/shard_map/ppermute | solution.py:19
  76.8 1.8 collective-permute-done.3
  78.9 30.5 %all-reduce.2 = bf16[256,1024]{1,0:T(8,128)(2,1)S(1)} all-reduce(f32[256,1024]{1,0:T(8,128)S(1)} %fusion.61), channel_id=1, replica_groups=mesh['tiles'=128,'samp'=4] {'samp'}, use_global_device_ids=true, to_apply=%region_0.1 | all-reduce | flops 262144 | bytes 1572864 | tf_op jit(solution)/shard_map/psum | solution.py:75
  109.4 1.9 collective-permute-start.4
  111.3 7.1 %collective-permute-start.5 = (bf16[256,1024]{1,0:T(8,128)(2,1)S(1)}, bf16[256,1024]{1,0:T(8,128)(2,1)S(1)}, u32[]{:S(2)}, u32[]{:S(2)}) collective-permute-start(bf16[256,1024]{1,0:T(8,128)(2,1)S(1)} %all-reduce.2), channel_id=1, source_target_pairs={{4,0},{8,4},{12,8},{16,12},{20,16},{24,20},{28,24},{32,28},{36,32}... | collective-permute-start | bytes 1572872 | tf_op jit(solution)/shard_map/ppermute | solution.py:20
  118.4 0.6 slice.416
  119.0 0.7 fusion.373
  134.6 0.6 copy-done
  136.3 0.9 add_dynamic-update-slice_fusion.10
  137.9 0.9 fusion.57
  138.8 0.5 multiply_select_fusion.7
  139.6 0.9 add_dynamic-update-slice_fusion.9
  141.2 0.8 add_dynamic-update-slice_fusion.8
  142.0 0.5 multiply_select_fusion.5
  142.8 0.8 add_dynamic-update-slice_fusion.7
  143.7 0.5 multiply_select_fusion.4
  144.4 0.8 add_dynamic-update-slice_fusion.6
  146.0 0.9 add_dynamic-update-slice_fusion.5
  146.9 0.5 multiply_select_fusion.2
  147.6 0.8 add_dynamic-update-slice_fusion.4
  148.4 0.5 multiply_select_fusion.1
  149.2 0.9 add_dynamic-update-slice_fusion.3
  151.3 0.8 add_dynamic-update-slice_fusion.2
  152.4 1.9 collective-permute-start.6
  154.3 7.0 %collective-permute-start.7 = (f32[256,1024]{1,0:T(8,128)S(1)}, f32[256,1024]{1,0:T(8,128)S(1)}, u32[]{:S(2)}, u32[]{:S(2)}) collective-permute-start(f32[256,1024]{1,0:T(8,128)S(1)} %get-tuple-element.6), channel_id=1, source_target_pairs={{4,0},{8,4},{12,8},{16,12},{20,16},{24,20},{28,24},{32,28},{36,32}... | collective-permute-start | bytes 3145736 | tf_op jit(solution)/shard_map/ppermute | solution.py:20
  161.3 10.5 %collective-permute-done.6 = f32[256,1024]{1,0:T(8,128)S(1)} collective-permute-done((f32[256,1024]{1,0:T(8,128)S(1)}, f32[256,1024]{1,0:T(8,128)S(1)}, u32[]{:S(2)}, u32[]{:S(2)}) %collective-permute-start.6) | collective-permute-done | bytes 1048608 | tf_op jit(solution)/shard_map/ppermute | solution.py:19
  171.8 1.8 collective-permute-done.7
  173.9 30.4 %all-reduce.3 = bf16[256,1024]{1,0:T(8,128)(2,1)S(1)} all-reduce(f32[256,1024]{1,0:T(8,128)S(1)} %fusion.60), channel_id=1, replica_groups=mesh['tiles'=128,'samp'=4] {'samp'}, use_global_device_ids=true, to_apply=%region_1.2 | all-reduce | flops 262144 | bytes 1572864 | tf_op jit(solution)/shard_map/psum | solution.py:75
  204.3 1.9 collective-permute-start.8
  206.2 7.2 %collective-permute-start.9 = (bf16[256,1024]{1,0:T(8,128)(2,1)S(1)}, bf16[256,1024]{1,0:T(8,128)(2,1)S(1)}, u32[]{:S(2)}, u32[]{:S(2)}) collective-permute-start(bf16[256,1024]{1,0:T(8,128)(2,1)S(1)} %all-reduce.3), channel_id=1, source_target_pairs={{4,0},{8,4},{12,8},{16,12},{20,16},{24,20},{28,24},{32,28},{36,32}... | collective-permute-start | bytes 1572872 | tf_op jit(solution)/shard_map/ppermute | solution.py:20
  213.4 4.7 %collective-permute-done.8 = bf16[256,1024]{1,0:T(8,128)(2,1)S(1)} collective-permute-done((bf16[256,1024]{1,0:T(8,128)(2,1)S(1)}, bf16[256,1024]{1,0:T(8,128)(2,1)S(1)}, u32[]{:S(2)}, u32[]{:S(2)}) %collective-permute-start.8) | collective-permute-done | bytes 524320 | tf_op jit(solution)/shard_map/ppermute | solution.py:19
  218.1 1.8 collective-permute-done.9
  222.2 0.5 bitcast_dynamic-update-slice_fusion.9
  223.3 0.5 bitcast_dynamic-update-slice_fusion.7
  223.8 0.5 bitcast_dynamic-update-slice_fusion.6
  224.3 0.5 bitcast_dynamic-update-slice_fusion.5
  224.9 0.5 bitcast_dynamic-update-slice_fusion.4
  225.9 0.5 bitcast_dynamic-update-slice_fusion.2
  226.4 0.5 bitcast_dynamic-update-slice_fusion.1
  226.9 1.5 copy-done.21
  228.4 1.2 bitcast_dynamic-update-slice_fusion
  (103 shorter events, 14.8 us)
Async XLA Ops:
  0.0 27.2 %copy-start.20 = (s32[10,2]{0,1:T(2,128)S(1)}, s32[10,2]{0,1:T(2,128)}, u32[]{:S(2)}) copy-start(s32[10,2]{0,1:T(2,128)} %param.5) | copy-start | bytes 244
  1.8 14.4 %all-to-all-start = ((bf16[4,64,1024]{2,1,0:T(8,128)(2,1)}), bf16[4,64,1024]{2,1,0:T(8,128)(2,1)S(1)}, u32[]{:S(2)}, u32[]{:S(2)}) async-start(bf16[4,64,1024]{2,1,0:T(8,128)(2,1)} %stack.62), calls=%async_computation | async-start | bytes 1048576 | tf_op jit(solution)/shard_map/all_to_all | solution.py:45
  16.2 27.7 %collective-permute-start = (bf16[256,1024]{1,0:T(8,128)(2,1)S(1)}, bf16[256,1024]{1,0:T(8,128)(2,1)S(1)}, u32[]{:S(2)}, u32[]{:S(2)}) collective-permute-start(bf16[256,1024]{1,0:T(8,128)(2,1)S(1)} %bitcast.161), channel_id=1, source_target_pairs={{0,4},{4,8},{8,12},{12,16},{16,20},{20,24},{24,28},{28,32},{32,36}... | collective-permute-start | bytes 1572872 | tf_op jit(solution)/shard_map/ppermute | solution.py:19
  18.1 26.6 %collective-permute-start.1 = (bf16[256,1024]{1,0:T(8,128)(2,1)S(1)}, bf16[256,1024]{1,0:T(8,128)(2,1)}, u32[]{:S(2)}, u32[]{:S(2)}) collective-permute-start(bf16[256,1024]{1,0:T(8,128)(2,1)S(1)} %bitcast.162), channel_id=1, source_target_pairs={{4,0},{8,4},{12,8},{16,12},{20,16},{24,20},{28,24},{32,28},{36,32}... | collective-permute-start | bytes 1572872 | tf_op jit(solution)/shard_map/ppermute | solution.py:20
  43.9 0.8 copy-start.19
  57.4 19.4 %collective-permute-start.2 = (f32[256,1024]{1,0:T(8,128)S(1)}, f32[256,1024]{1,0:T(8,128)S(1)}, u32[]{:S(2)}, u32[]{:S(2)}) collective-permute-start(f32[256,1024]{1,0:T(8,128)S(1)} %get-tuple-element.7), channel_id=1, source_target_pairs={{0,4},{4,8},{8,12},{12,16},{16,20},{20,24},{24,28},{28,32},{32,36}... | collective-permute-start | bytes 3145736 | tf_op jit(solution)/shard_map/ppermute | solution.py:19
  59.3 19.3 %collective-permute-start.3 = (f32[256,1024]{1,0:T(8,128)S(1)}, f32[256,1024]{1,0:T(8,128)S(1)}, u32[]{:S(2)}, u32[]{:S(2)}) collective-permute-start(f32[256,1024]{1,0:T(8,128)S(1)} %get-tuple-element.8), channel_id=1, source_target_pairs={{4,0},{8,4},{12,8},{16,12},{20,16},{24,20},{28,24},{32,28},{36,32}... | collective-permute-start | bytes 3145736 | tf_op jit(solution)/shard_map/ppermute | solution.py:20
  109.4 22.8 %collective-permute-start.4 = (bf16[256,1024]{1,0:T(8,128)(2,1)S(1)}, bf16[256,1024]{1,0:T(8,128)(2,1)S(1)}, u32[]{:S(2)}, u32[]{:S(2)}) collective-permute-start(bf16[256,1024]{1,0:T(8,128)(2,1)S(1)} %all-reduce.2), channel_id=1, source_target_pairs={{0,4},{4,8},{8,12},{12,16},{16,20},{20,24},{24,28},{28,32},{32,36}... | collective-permute-start | bytes 1572872 | tf_op jit(solution)/shard_map/ppermute | solution.py:19
  111.3 20.9 %collective-permute-start.5 = (bf16[256,1024]{1,0:T(8,128)(2,1)S(1)}, bf16[256,1024]{1,0:T(8,128)(2,1)S(1)}, u32[]{:S(2)}, u32[]{:S(2)}) collective-permute-start(bf16[256,1024]{1,0:T(8,128)(2,1)S(1)} %all-reduce.2), channel_id=1, source_target_pairs={{4,0},{8,4},{12,8},{16,12},{20,16},{24,20},{28,24},{32,28},{36,32}... | collective-permute-start | bytes 1572872 | tf_op jit(solution)/shard_map/ppermute | solution.py:20
  133.5 1.7 copy-start
  137.6 1.7 copy-start.3
  139.3 1.6 copy-start.5
  140.9 1.6 copy-start.7
  142.6 1.6 copy-start.9
  144.2 1.5 copy-start.11
  145.7 1.7 copy-start.13
  147.4 1.5 copy-start.15
  148.9 1.7 copy-start.17
  150.6 0.7 copy-start.1
  152.4 19.4 %collective-permute-start.6 = (f32[256,1024]{1,0:T(8,128)S(1)}, f32[256,1024]{1,0:T(8,128)S(1)}, u32[]{:S(2)}, u32[]{:S(2)}) collective-permute-start(f32[256,1024]{1,0:T(8,128)S(1)} %get-tuple-element.5), channel_id=1, source_target_pairs={{0,4},{4,8},{8,12},{12,16},{16,20},{20,24},{24,28},{28,32},{32,36}... | collective-permute-start | bytes 3145736 | tf_op jit(solution)/shard_map/ppermute | solution.py:19
  154.3 19.3 %collective-permute-start.7 = (f32[256,1024]{1,0:T(8,128)S(1)}, f32[256,1024]{1,0:T(8,128)S(1)}, u32[]{:S(2)}, u32[]{:S(2)}) collective-permute-start(f32[256,1024]{1,0:T(8,128)S(1)} %get-tuple-element.6), channel_id=1, source_target_pairs={{4,0},{8,4},{12,8},{16,12},{20,16},{24,20},{28,24},{32,28},{36,32}... | collective-permute-start | bytes 3145736 | tf_op jit(solution)/shard_map/ppermute | solution.py:20
  204.3 13.8 %collective-permute-start.8 = (bf16[256,1024]{1,0:T(8,128)(2,1)S(1)}, bf16[256,1024]{1,0:T(8,128)(2,1)S(1)}, u32[]{:S(2)}, u32[]{:S(2)}) collective-permute-start(bf16[256,1024]{1,0:T(8,128)(2,1)S(1)} %all-reduce.3), channel_id=1, source_target_pairs={{0,4},{4,8},{8,12},{12,16},{16,20},{20,24},{24,28},{28,32},{32,36}... | collective-permute-start | bytes 1572872 | tf_op jit(solution)/shard_map/ppermute | solution.py:19
  206.2 13.6 %collective-permute-start.9 = (bf16[256,1024]{1,0:T(8,128)(2,1)S(1)}, bf16[256,1024]{1,0:T(8,128)(2,1)S(1)}, u32[]{:S(2)}, u32[]{:S(2)}) collective-permute-start(bf16[256,1024]{1,0:T(8,128)(2,1)S(1)} %all-reduce.3), channel_id=1, source_target_pairs={{4,0},{8,4},{12,8},{16,12},{20,16},{24,20},{28,24},{32,28},{36,32}... | collective-permute-start | bytes 1572872 | tf_op jit(solution)/shard_map/ppermute | solution.py:20
  221.5 1.2 copy-start.4
  222.0 1.3 copy-start.6
  222.8 1.0 copy-start.8
  223.3 1.0 copy-start.10
  223.8 1.0 copy-start.12
  224.3 1.0 copy-start.14
  224.9 1.0 copy-start.16
  225.4 1.0 copy-start.18
  225.9 2.5 %copy-start.2 = (f32[128,512]{1,0:T(8,128)S(1)}, f32[128,512]{1,0:T(8,128)}, u32[]{:S(2)}) copy-start(f32[128,512]{1,0:T(8,128)} %copy-done.1) | copy-start | bytes 786436
  226.9 1.5 copy-start.21
